TPU v7x, 512 devices: a whole 4x8x8 slice. The times are simulated.
512 devices in a mesh: blk: 16 (over x, y_hi, core), wide: 32 (over y_lo, z).
Axes of the slice: x: 4, y: 8 (y_hi: 2, y_lo: 4; y = y_hi * 4 + y_lo), z: 8, core: 2. Of those that a mesh axis runs over, the one named last changes fastest.
Arguments:
- observed: bfloat16 [131072, 5120], P(('blk', 'wide')), may hold values from -8 to 8
- mask_bits: int32 [131072, 640], P(('blk', 'wide')), may hold values from 0 to 255, as said below
- frame_factors: float32 [131072, 256], P(('blk', 'wide')), may hold values from -2 to 2
- pixel_factors: bfloat16 [524288, 256], P(('blk', 'wide')), may hold values from -2 to 2
Outputs:
- frames_out: float32 [131072, 256], P(('blk', 'wide'))
- pixels_out: bfloat16 [524288, 256], P(('blk', 'wide'))
Inputs may be any that keep to these rules, and one draw needn't show every extreme that they name: `mask_bits`: each word holds 8 independent flags, each set with probability one half.
All inputs are finite; a program needn't handle non-finite values.
Results may differ from a plain program's by a relative error of at most 0.0071.
Values may be sent and summed in bfloat16 or wider, within the bound.
A program may use at most 64 MiB of HBM per device.

v0:
```python
import jax
import jax.numpy as jnp
from jax import lax
from jax.sharding import PartitionSpec as P

VISITS = 5


clip_level = 1.0
step_frames = 0.01
step_pixels = 0.02
decay_weight = 0.1


def shifted(value, axis, steps):
    count = lax.axis_size(axis)
    pairs = [(source, (source + steps) % count) for source in range(count)]
    return lax.ppermute(value, axis, pairs)


def unpack_mask(packed):
    shifts = jnp.arange(8, dtype=jnp.int32)
    expanded = jnp.bitwise_and(jnp.right_shift(packed[..., None, :], shifts[:, None]), 1)
    return expanded.reshape(packed.shape[:-1] + (8 * packed.shape[-1],)).astype(jnp.float32)


def send_block(block, visit_index):
    if visit_index < VISITS - 2:
        return shifted(block, "blk", 1)
    if visit_index == VISITS - 2:
        return shifted(block, "wide", 1)
    return block


def body(observed, mask_bits, frame_factors, pixel_factors):
    visible_all = unpack_mask(mask_bits).astype(jnp.bfloat16)
    frames = frame_factors
    pixels = pixel_factors
    width = pixels.shape[0]
    for visit_index in range(VISITS):
        lower = visit_index * width
        wanted = observed[:, lower : lower + width].astype(jnp.float32)
        visible = visible_all[:, lower : lower + width].astype(jnp.float32)
        frames_low = frames.astype(jnp.bfloat16)
        predicted = jnp.dot(frames_low, pixels.T, preferred_element_type=jnp.float32)
        errors = visible * (wanted - predicted)
        weights = clip_level / jnp.maximum(jnp.abs(errors), clip_level)
        scaled = (weights * errors).astype(jnp.bfloat16)
        grad = jnp.dot(scaled, pixels, preferred_element_type=jnp.float32)
        new_frames = frames + step_frames * (grad - decay_weight * frames)
        pixel_grad = lax.dot_general(
            scaled, frames_low, (((0,), (0,)), ((), ())), preferred_element_type=jnp.float32
        )
        current = pixels.astype(jnp.float32)
        moved = send_block(
            (current + step_pixels * (pixel_grad - decay_weight * current)).astype(jnp.bfloat16),
            visit_index,
        )
        frames = new_frames
        pixels = moved
    return (frames, pixels)


def solution(mesh):
    in_specs = (
        P(("blk", "wide"), None),
        P(("blk", "wide"), None),
        P(("blk", "wide"), None),
        P(("blk", "wide"), None),
    )
    out_specs = (P(("blk", "wide"), None), P(("blk", "wide"), None))
    return jax.shard_map(body, mesh=mesh, in_specs=in_specs, out_specs=out_specs, check_vma=False)
```

profile of v0, /device:TPU:16, one launch (start us, length us, event | category | flops | bytes accessed | tf_op | source)
XLA Modules:
  0.0 99.9 jit_solution(8195755883896972366)
XLA Ops:
  0.6 1.4 %shift_right_arithmetic.20 = s32[256,8,640]{2,1,0:T(8,128)S(1)} broadcast(s32[256,640]{1,0:T(8,128)} %param.5), dimensions={0,2} | broadcast | bytes 5898240 | tf_op jit(solution)/shard_map/shift_right_arithmetic | solution.py:23
  2.1 3.2 %copy.6 = s32[32,8,8,640]{3,1,2,0:T(8,128)} copy(s32[32,8,8,640]{3,2,1,0:T(8,128)S(1)} %bitcast.23) | data formatting | bytes 10485760
  5.3 0.0 copy-start
  5.3 0.0 copy-start.1
  5.3 0.0 copy-start.2
  5.3 3.3 %convert_convert_fusion = bf16[256,5120]{1,0:T(8,128)(2,1)S(1)} fusion(s32[256,5120]{1,0:T(8,128)} %bitcast.22, s32[5120]{0:T(1024)S(1)} %shift_right_arithmetic.23), kind=kLoop, calls=%fused_computation | loop fusion | flops 5242880 | bytes 7884800 | tf_op jit(solution)/shard_map/convert_element_type | solution.py:36
  8.7 0.0 copy-done
  8.7 0.0 copy-done.1
  8.7 0.2 copy-done.2
  8.8 0.5 multiply_convert_fusion.4
  9.3 0.4 fusion.7
  9.8 1.9 %collective-permute-start = (bf16[1024,256]{1,0:T(8,128)(2,1)S(1)}, bf16[1024,256]{1,0:T(8,128)(2,1)S(1)}, u32[]{:S(2)}, u32[]{:S(2)}) collective-permute-start(bf16[1024,256]{1,0:T(8,128)(2,1)S(1)} %fusion.7), channel_id=1, source_target_pairs={{0,32},{32,64},{64,96},{96,128},{128,160},{160,192},{192,224},{224... | collective-permute-start | bytes 1572872 | tf_op jit(solution)/shard_map/ppermute | solution.py:18
  11.7 0.3 fusion.9
  12.0 14.4 %collective-permute-done = bf16[1024,256]{1,0:T(8,128)(2,1)S(1)} collective-permute-done((bf16[1024,256]{1,0:T(8,128)(2,1)S(1)}, bf16[1024,256]{1,0:T(8,128)(2,1)S(1)}, u32[]{:S(2)}, u32[]{:S(2)}) %collective-permute-start) | collective-permute-done | bytes 524320 | tf_op jit(solution)/shard_map/ppermute | solution.py:18
  26.4 0.5 multiply_convert_fusion.3
  26.9 0.4 fusion.20
  27.3 3.1 %collective-permute-start.1 = (bf16[1024,256]{1,0:T(8,128)(2,1)S(1)}, bf16[1024,256]{1,0:T(8,128)(2,1)S(1)}, u32[]{:S(2)}, u32[]{:S(2)}) collective-permute-start(bf16[1024,256]{1,0:T(8,128)(2,1)S(1)} %fusion.20), channel_id=1, source_target_pairs={{0,32},{32,64},{64,96},{96,128},{128,160},{160,192},{192,224},{224... | collective-permute-start | bytes 1572872 | tf_op jit(solution)/shard_map/ppermute | solution.py:18
  30.4 0.3 fusion.11
  30.7 13.2 %collective-permute-done.1 = bf16[1024,256]{1,0:T(8,128)(2,1)S(1)} collective-permute-done((bf16[1024,256]{1,0:T(8,128)(2,1)S(1)}, bf16[1024,256]{1,0:T(8,128)(2,1)S(1)}, u32[]{:S(2)}, u32[]{:S(2)}) %collective-permute-start.1) | collective-permute-done | bytes 524320 | tf_op jit(solution)/shard_map/ppermute | solution.py:18
  43.9 0.5 multiply_convert_fusion.2
  44.4 0.4 fusion.23
  44.9 4.4 %collective-permute-start.2 = (bf16[1024,256]{1,0:T(8,128)(2,1)S(1)}, bf16[1024,256]{1,0:T(8,128)(2,1)S(1)}, u32[]{:S(2)}, u32[]{:S(2)}) collective-permute-start(bf16[1024,256]{1,0:T(8,128)(2,1)S(1)} %fusion.23), channel_id=1, source_target_pairs={{0,32},{32,64},{64,96},{96,128},{128,160},{160,192},{192,224},{224... | collective-permute-start | bytes 1572872 | tf_op jit(solution)/shard_map/ppermute | solution.py:18
  49.2 0.3 fusion.13
  49.5 11.9 %collective-permute-done.2 = bf16[1024,256]{1,0:T(8,128)(2,1)S(1)} collective-permute-done((bf16[1024,256]{1,0:T(8,128)(2,1)S(1)}, bf16[1024,256]{1,0:T(8,128)(2,1)S(1)}, u32[]{:S(2)}, u32[]{:S(2)}) %collective-permute-start.2) | collective-permute-done | bytes 524320 | tf_op jit(solution)/shard_map/ppermute | solution.py:18
  61.5 0.5 multiply_convert_fusion.1
  62.0 0.4 fusion.26
  62.4 12.9 %collective-permute-start.3 = (bf16[1024,256]{1,0:T(8,128)(2,1)S(1)}, bf16[1024,256]{1,0:T(8,128)(2,1)S(1)}, u32[]{:S(2)}, u32[]{:S(2)}) collective-permute-start(bf16[1024,256]{1,0:T(8,128)(2,1)S(1)} %fusion.26), channel_id=1, source_target_pairs={{0,1},{1,2},{2,3},{3,4},{4,5},{5,6},{6,7},{7,8},{8,9},{9,10},{10,1... | collective-permute-start | bytes 1572872 | tf_op jit(solution)/shard_map/ppermute | solution.py:18
  75.3 0.3 fusion.15
  75.6 21.6 %collective-permute-done.3 = bf16[1024,256]{1,0:T(8,128)(2,1)S(1)} collective-permute-done((bf16[1024,256]{1,0:T(8,128)(2,1)S(1)}, bf16[1024,256]{1,0:T(8,128)(2,1)S(1)}, u32[]{:S(2)}, u32[]{:S(2)}) %collective-permute-start.3) | collective-permute-done | bytes 524320 | tf_op jit(solution)/shard_map/ppermute | solution.py:18
  97.2 0.5 multiply_convert_fusion
  97.7 1.2 %fusion.29 = bf16[1024,256]{1,0:T(8,128)(2,1)} fusion(bf16[1024,256]{1,0:T(8,128)(2,1)S(1)} %collective-permute-done.3, bf16[256,1024]{1,0:T(8,128)(2,1)S(1)} %multiply_convert_fusion, f32[256,256]{1,0:T(8,128)S(1)} %fusion.15), kind=kOutput, calls=%fused_computation.50 | convolution fusion | flops 135856128 | bytes 1835008 | tf_op jit(solution)/shard_map/dot_general | solution.py:51
  98.9 1.0 %fusion.17 = f32[256,256]{1,0:T(8,128)} fusion(f32[256,256]{1,0:T(8,128)S(1)} %fusion.15, bf16[256,1024]{1,0:T(8,128)(2,1)S(1)} %multiply_convert_fusion, bf16[1024,256]{1,0:T(8,128)(2,1)S(1)} %collective-permute-done.3), kind=kOutput, calls=%fused_computation.38 | convolution fusion | flops 134479872 | bytes 1572864 | tf_op jit(solution)/shard_map/dot_general | solution.py:49
  (2 shorter events, 0.0 us)
Async XLA Ops:
  5.3 3.4 %copy-start = (bf16[1024,256]{1,0:T(8,128)(2,1)S(1)}, bf16[1024,256]{1,0:T(8,128)(2,1)}, u32[]{:S(2)}) copy-start(bf16[1024,256]{1,0:T(8,128)(2,1)} %param.7) | copy-start | bytes 1572868
  5.3 3.4 %copy-start.1 = (f32[256,256]{1,0:T(8,128)S(1)}, f32[256,256]{1,0:T(8,128)}, u32[]{:S(2)}) copy-start(f32[256,256]{1,0:T(8,128)} %param.6) | copy-start | bytes 786436
  5.3 3.5 %copy-start.2 = (bf16[256,5120]{1,0:T(8,128)(2,1)S(1)}, bf16[256,5120]{1,0:T(8,128)(2,1)}, u32[]{:S(2)}) copy-start(bf16[256,5120]{1,0:T(8,128)(2,1)} %param.4) | copy-start | bytes 7864324
  9.8 16.6 %collective-permute-start = (bf16[1024,256]{1,0:T(8,128)(2,1)S(1)}, bf16[1024,256]{1,0:T(8,128)(2,1)S(1)}, u32[]{:S(2)}, u32[]{:S(2)}) collective-permute-start(bf16[1024,256]{1,0:T(8,128)(2,1)S(1)} %fusion.7), channel_id=1, source_target_pairs={{0,32},{32,64},{64,96},{96,128},{128,160},{160,192},{192,224},{224... | collective-permute-start | bytes 1572872 | tf_op jit(solution)/shard_map/ppermute | solution.py:18
  27.3 16.6 %collective-permute-start.1 = (bf16[1024,256]{1,0:T(8,128)(2,1)S(1)}, bf16[1024,256]{1,0:T(8,128)(2,1)S(1)}, u32[]{:S(2)}, u32[]{:S(2)}) collective-permute-start(bf16[1024,256]{1,0:T(8,128)(2,1)S(1)} %fusion.20), channel_id=1, source_target_pairs={{0,32},{32,64},{64,96},{96,128},{128,160},{160,192},{192,224},{224... | collective-permute-start | bytes 1572872 | tf_op jit(solution)/shard_map/ppermute | solution.py:18
  44.9 16.6 %collective-permute-start.2 = (bf16[1024,256]{1,0:T(8,128)(2,1)S(1)}, bf16[1024,256]{1,0:T(8,128)(2,1)S(1)}, u32[]{:S(2)}, u32[]{:S(2)}) collective-permute-start(bf16[1024,256]{1,0:T(8,128)(2,1)S(1)} %fusion.23), channel_id=1, source_target_pairs={{0,32},{32,64},{64,96},{96,128},{128,160},{160,192},{192,224},{224... | collective-permute-start | bytes 1572872 | tf_op jit(solution)/shard_map/ppermute | solution.py:18
  62.4 34.8 %collective-permute-start.3 = (bf16[1024,256]{1,0:T(8,128)(2,1)S(1)}, bf16[1024,256]{1,0:T(8,128)(2,1)S(1)}, u32[]{:S(2)}, u32[]{:S(2)}) collective-permute-start(bf16[1024,256]{1,0:T(8,128)(2,1)S(1)} %fusion.26), channel_id=1, source_target_pairs={{0,1},{1,2},{2,3},{3,4},{4,5},{5,6},{6,7},{7,8},{8,9},{9,10},{10,1... | collective-permute-start | bytes 1572872 | tf_op jit(solution)/shard_map/ppermute | solution.py:18
where the time goes:
time: 100 us; the launch traced here: 99.9 us
  waiting for transfers between devices  61.1 us (61%)
  starting transfers between devices  22.2 us (22%)
  matrix products  7.57 us (8%)
  local copies, waits for them, and re-layouts  4.85 us (5%)
  other arithmetic  3.32 us (3%)
    ppermute x4, waiting for transfers between devices, shifted(): return lax.ppermute(value, axis, pairs)  61.1 us
    ppermute x4, starting transfers between devices, shifted(): return lax.ppermute(value, axis, pairs)  22.2 us
    unnamed x7, local copies, waits for them, and re-layouts  3.41 us
    convert_element_type x1, other arithmetic, body(): visible_all = unpack_mask(mask_bits).astype(jnp.bfloat16)  3.32 us
    dot_general x5, matrix products, body(): lax.dot_general(scaled, frames_low, (((0,), (0,)), ((), ())), preferred_e...  2.87 us
    dot_general x5, matrix products, body(): jnp.dot(frames_low, pixels.T, preferred_element_type=jnp.float32)  2.48 us
    dot_general x5, matrix products, body(): grad = jnp.dot(scaled, pixels, preferred_element_type=jnp.float32)  2.22 us
  transfers between devices with their start and end apart: 4, of which 4 were waited for; matrix products, arithmetic and copies ran while one was open for 1% of the time, Pallas kernels for 0%

commit v1 on v0

v1 whole, which is shorter than its diff:
```python
import functools

import jax
import jax.numpy as jnp
from jax import lax
from jax.experimental import pallas as pl
from jax.experimental.pallas import tpu as pltpu
from jax.sharding import PartitionSpec as P

VISITS = 5
LANES = 128
CHUNK = 128
MESH = pl.DeviceIdType.MESH

step_frames = 0.01
step_pixels = 0.02
decay_weight = 0.1


def kernel(
    n_blk, n_wide, obs_hbm, bits_hbm, frames_hbm, pixels_hbm, frames_out, pixels_out,
    obs, bits, frames, low, total, held, fresh, load_sem, send_sem, recv_sem,
):
    width = pixels_out.shape[0]
    chunks = width // CHUNK
    groups = bits.shape[1] // LANES
    i, j = lax.axis_index("blk"), lax.axis_index("wide")
    next_blk = (lax.rem(i + 1, n_blk), j)
    last_blk = (lax.rem(i + n_blk - 1, n_blk), j)
    next_wide = (i, lax.rem(j + 1, n_wide))
    last_wide = (i, lax.rem(j + n_wide - 1, n_wide))

    barrier = pltpu.get_barrier_semaphore()
    for peer in (next_blk, last_blk, next_wide, last_wide):
        pl.semaphore_signal(barrier, inc=1, device_id=peer, device_id_type=MESH)

    def load(source, target, index):
        return pltpu.make_async_copy(source, target, load_sem.at[index])

    def load_obs(visit):
        columns = pl.ds(visit * width, width)
        return load(obs_hbm.at[:, columns], obs.at[:, columns], 3 + visit)

    first = [load(frames_hbm, frames, 0), load(pixels_hbm, held.at[0], 1), load(bits_hbm, bits, 2)]
    for copy in first:
        copy.start()
    for visit in range(VISITS):
        load_obs(visit).start()
    for copy in first:
        copy.wait()

    def send(visit, chunk):
        rows = pl.ds(pl.multiple_of(chunk * CHUNK, CHUNK), CHUNK)
        return pltpu.make_async_remote_copy(
            src_ref=fresh.at[visit, rows],
            dst_ref=held.at[visit + 1, rows],
            send_sem=send_sem.at[visit, chunk],
            recv_sem=recv_sem.at[visit, chunk],
            device_id=next_blk if visit < VISITS - 2 else next_wide,
            device_id_type=MESH,
        )

    def update(visit, chunk):
        rows = pl.ds(pl.multiple_of(chunk * CHUNK, CHUNK), CHUNK)
        old = held[visit, rows, :]
        low_frames = low[...]
        predicted = lax.dot_general(
            low_frames, old, (((1,), (1,)), ((), ())), preferred_element_type=jnp.float32
        )
        place = visit * (width // LANES) + chunk
        columns = pl.ds(pl.multiple_of(place * LANES, LANES), LANES)
        words = bits[:, pl.ds(pl.multiple_of(lax.rem(place, groups) * LANES, LANES), LANES)]
        flag = jnp.left_shift(jnp.int32(1), lax.div(place, groups))
        errors = jnp.where((words & flag) != 0, obs[:, columns].astype(jnp.float32) - predicted, 0.0)
        scaled = jnp.clip(errors, -1.0, 1.0).astype(jnp.bfloat16)
        total[...] += jnp.dot(scaled, old, preferred_element_type=jnp.float32)
        grad = lax.dot_general(
            scaled, low_frames, (((0,), (0,)), ((), ())), preferred_element_type=jnp.float32
        )
        wide_old = old.astype(jnp.float32)
        new = (wide_old + step_pixels * (grad - decay_weight * wide_old)).astype(jnp.bfloat16)
        if visit < VISITS - 1:
            fresh[visit, rows, :] = new
        else:
            pixels_out[rows, :] = new

    for visit in range(VISITS):
        low[...] = frames[...].astype(jnp.bfloat16)
        total[...] = jnp.zeros_like(total)
        load_obs(visit).wait()

        if visit == 0:
            @pl.loop(0, chunks)
            def _(chunk):
                update(0, chunk)

            pl.semaphore_wait(barrier, 4)

            @pl.loop(0, chunks)
            def _(chunk):
                send(0, chunk).start()
        else:
            @pl.loop(0, chunks)
            def _(chunk, visit=visit):
                send(visit - 1, chunk).wait_recv()
                update(visit, chunk)
                if visit < VISITS - 1:
                    send(visit, chunk).start()

        current = frames[...]
        updated = current + step_frames * (total[...] - decay_weight * current)
        if visit < VISITS - 1:
            frames[...] = updated
        else:
            frames_out[...] = updated

    for visit in range(VISITS - 1):
        @pl.loop(0, chunks)
        def _(chunk, visit=visit):
            send(visit, chunk).wait_send()


def solution(mesh):
    n_blk, n_wide = mesh.shape["blk"], mesh.shape["wide"]

    def body(observed, mask_bits, frame_factors, pixel_factors):
        width, rank = pixel_factors.shape
        chunks = width // CHUNK
        return tuple(pl.pallas_call(
            functools.partial(kernel, n_blk, n_wide),
            out_shape=(
                jax.ShapeDtypeStruct(frame_factors.shape, frame_factors.dtype),
                jax.ShapeDtypeStruct(pixel_factors.shape, pixel_factors.dtype),
            ),
            in_specs=[pl.BlockSpec(memory_space=pl.ANY)] * 4,
            out_specs=(pl.BlockSpec(memory_space=pltpu.VMEM),) * 2,
            scratch_shapes=[
                pltpu.VMEM(observed.shape, observed.dtype),
                pltpu.VMEM(mask_bits.shape, mask_bits.dtype),
                pltpu.VMEM(frame_factors.shape, jnp.float32),
                pltpu.VMEM(frame_factors.shape, jnp.bfloat16),
                pltpu.VMEM(frame_factors.shape, jnp.float32),
                pltpu.VMEM((VISITS, width, rank), jnp.bfloat16),
                pltpu.VMEM((VISITS - 1, width, rank), jnp.bfloat16),
                pltpu.SemaphoreType.DMA((3 + VISITS,)),
                pltpu.SemaphoreType.DMA((VISITS - 1, chunks)),
                pltpu.SemaphoreType.DMA((VISITS - 1, chunks)),
            ],
            compiler_params=pltpu.CompilerParams(
                collective_id=0, has_side_effects=True
            ),
        )(observed, mask_bits, frame_factors, pixel_factors))

    spec = P(("blk", "wide"), None)
    return jax.shard_map(
        body, mesh=mesh, in_specs=(spec,) * 4, out_specs=(spec, spec), check_vma=False
    )
```

time: 100 us -> 72.5 us (0.72)
  Pallas kernels: 0 us -> 68.1 us
  waiting for transfers between devices: 61.1 us -> 0 us
  starting transfers between devices: 22.2 us -> 0 us
  matrix products: 7.57 us -> 0 us
  other arithmetic: 3.32 us -> 0 us
  local copies, waits for them, and re-layouts: 4.85 us -> 3.54 us
    pallas_call x0 -> x1, Pallas kernels: none -> 68.1 us  [body(): pl.pallas_call(functools.partial(kernel, n_blk, n_wide), out_shape=(jax.S...]
    ppermute x4 -> x0, waiting for transfers between devices: 61.1 us -> none  [shifted(): return lax.ppermute(value, axis, pairs)]
    ppermute x4 -> x0, starting transfers between devices: 22.2 us -> none  [shifted(): return lax.ppermute(value, axis, pairs)]
    dot_general x15 -> x0, matrix products: 7.57 us -> none  [the longest x5 2.87 us: body(): lax.dot_general(scaled, frames_low, (((0,), (0,)), ((), ())), preferred_e...]
    convert_element_type x1 -> x0, other arithmetic: 3.32 us -> none  [body(): visible_all = unpack_mask(mask_bits).astype(jnp.bfloat16)]
    shift_right_arithmetic x3 -> x0, local copies, waits for them, and re-layouts: 1.44 us -> none  [unpack_mask(): jnp.right_shift(packed[..., None, :], shifts[:, None])]
    unnamed x7 -> x2, local copies, waits for them, and re-layouts: 3.41 us -> 3.54 us
  transfers between devices with their start and end apart: 4 -> 0, of which waited for: 4 -> 0; matrix products, arithmetic and copies ran while one was open for 1% -> 0% of each run, Pallas kernels for 0% -> 0%
where the time goes in v1:
time: 72.5 us; the launch traced here: 72.3 us
  Pallas kernels  68.1 us (94%)
  local copies, waits for them, and re-layouts  3.54 us (5%)
    pallas_call x1, Pallas kernels, body(): pl.pallas_call(functools.partial(kernel, n_blk, n_wide), out_shape=(jax.S...  68.1 us
    unnamed x2, local copies, waits for them, and re-layouts  3.54 us

profile of v1, /device:TPU:16, one launch (start us, length us, event | category | flops | bytes accessed | tf_op | source)
XLA Modules:
  0.0 72.3 jit_solution(1950721392237562064)
XLA Ops:
  0.6 68.1 %shard_map.59 = (f32[256,256]{1,0:T(8,128)}, bf16[1024,256]{1,0:T(8,128)(2,1)}) custom-call(bf16[256,5120]{1,0:T(8,128)(2,1)} %obs_hbm.1, s32[256,640]{1,0:T(8,128)} %bits_hbm.1, f32[256,256]{1,0:T(8,128)} %frames_hbm.1, bf16[1024,256]{1,0:T(8,128)(2,1)} %pixels_hbm.1), custom_call_target="tpu_custom_call" | custom-call | tf_op jit(solution)/shard_map/pallas_call | solution.py:129
  68.7 1.7 %copy.8 = f32[256,256]{1,0:T(8,128)} copy(f32[256,256]{1,0:T(8,128)} %get-tuple-element.4) | data formatting | bytes 524288
  70.4 1.9 %copy.9 = bf16[1024,256]{1,0:T(8,128)(2,1)} copy(bf16[1024,256]{1,0:T(8,128)(2,1)} %get-tuple-element.5) | data formatting | bytes 1048576

commit v2 on v1

--- a/solution.py
+++ b/solution.py
@@ -10,6 +10,11 @@
 VISITS = 5
 LANES = 128
 CHUNK = 128
+RUN = 8
+RELAYED = 8
+AHEAD = 5
+GBASE = 5
+GUESTS = 3
 MESH = pl.DeviceIdType.MESH
 
 step_frames = 0.01
@@ -19,7 +24,8 @@
 
 def kernel(
     n_blk, n_wide, obs_hbm, bits_hbm, frames_hbm, pixels_hbm, frames_out, pixels_out,
-    obs, bits, frames, low, total, held, fresh, load_sem, send_sem, recv_sem,
+    obs, bits, frames, low, total, held, fresh, relay, load_sem, send_sem, recv_sem, relay_send, relay_recv,
+    guest, guest_send, guest_recv,
 ):
     width = pixels_out.shape[0]
     chunks = width // CHUNK
@@ -27,12 +33,53 @@
     i, j = lax.axis_index("blk"), lax.axis_index("wide")
     next_blk = (lax.rem(i + 1, n_blk), j)
     last_blk = (lax.rem(i + n_blk - 1, n_blk), j)
-    next_wide = (i, lax.rem(j + 1, n_wide))
-    last_wide = (i, lax.rem(j + n_wide - 1, n_wide))
+    place = lax.rem(j, RUN)
+    is_first, is_last = place == 0, place == RUN - 1
+    next_wide = (i, jnp.where(is_last, j - (RUN - 1), j + 1))
+    last_wide = (i, jnp.where(is_first, j + (RUN - 1), j - 1))
+    next_run = (i, lax.rem(j + RUN, n_wide))
+    last_run = (i, lax.rem(j + n_wide - RUN, n_wide))
+    right = (i, lax.rem(j + 1, n_wide))
+    left = (i, lax.rem(j + n_wide - 1, n_wide))
 
     barrier = pltpu.get_barrier_semaphore()
-    for peer in (next_blk, last_blk, next_wide, last_wide):
+
+    def greet(peer):
         pl.semaphore_signal(barrier, inc=1, device_id=peer, device_id_type=MESH)
+
+    greet(last_blk)
+
+    @pl.when(jnp.logical_not(is_first))
+    def _():
+        greet(left)
+
+    odd = lax.rem(i, 2) == 1
+    even = jnp.logical_not(odd)
+    is_host = even & (place < RUN - 1) & (place >= RUN - 1 - GUESTS)
+    guest_slot = jnp.where(is_host, RUN - 2 - place, 0)
+    guest_from = (lax.rem(i + 1, n_blk), jnp.where(is_host, j + guest_slot + 1, j))
+    guest_to = (lax.rem(i + 2, n_blk), guest_from[1])
+
+    def host_of(chunk):
+        return (lax.rem(i + n_blk - 1, n_blk), jnp.where(is_last, j - 1 - chunk, j))
+
+    @pl.when(is_host)
+    def _():
+        greet(guest_from)
+
+    @pl.when(is_last & even)
+    def _():
+        for chunk in range(GUESTS):
+            greet((lax.rem(i + n_blk - 2, n_blk), host_of(chunk)[1]))
+
+    @pl.when(is_first)
+    def _():
+        greet(last_wide)
+        greet(last_run)
+
+    def meet():
+        extra = jnp.where(is_host | is_first, 1, jnp.where(is_last & odd, GUESTS, 0))
+        pl.semaphore_wait(barrier, 2 + extra)
 
     def load(source, target, index):
         return pltpu.make_async_copy(source, target, load_sem.at[index])
@@ -56,9 +103,88 @@
             dst_ref=held.at[visit + 1, rows],
             send_sem=send_sem.at[visit, chunk],
             recv_sem=recv_sem.at[visit, chunk],
-            device_id=next_blk if visit < VISITS - 2 else next_wide,
-            device_id_type=MESH,
-        )
+            device_id=next_blk if visit < VISITS - 2 else right,
+            device_id_type=MESH,
+        )
+
+    def send_around(chunk):
+        chunk = jnp.minimum(chunk, RELAYED - 1)
+        rows = pl.ds(pl.multiple_of(chunk * CHUNK, CHUNK), CHUNK)
+        return pltpu.make_async_remote_copy(
+            src_ref=fresh.at[VISITS - 2, rows],
+            dst_ref=relay.at[rows],
+            send_sem=send_sem.at[VISITS - 2, chunk],
+            recv_sem=relay_recv.at[chunk],
+            device_id=next_wide,
+            device_id_type=MESH,
+        )
+
+    def pass_on(chunk):
+        rows = pl.ds(pl.multiple_of(chunk * CHUNK, CHUNK), CHUNK)
+        return pltpu.make_async_remote_copy(
+            src_ref=relay.at[rows],
+            dst_ref=held.at[VISITS - 1, rows],
+            send_sem=relay_send.at[chunk],
+            recv_sem=recv_sem.at[VISITS - 2, chunk],
+            device_id=next_run,
+            device_id_type=MESH,
+        )
+
+    def send_guest(visit, slot):
+        chunk = slot + GBASE
+        rows = pl.ds(pl.multiple_of(chunk * CHUNK, CHUNK), CHUNK)
+        return pltpu.make_async_remote_copy(
+            src_ref=fresh.at[visit, rows],
+            dst_ref=guest.at[visit],
+            send_sem=send_sem.at[visit, chunk],
+            recv_sem=guest_recv.at[visit],
+            device_id=host_of(slot),
+            device_id_type=MESH,
+        )
+
+    def guest_on(visit):
+        chunk = guest_slot + GBASE
+        rows = pl.ds(pl.multiple_of(chunk * CHUNK, CHUNK), CHUNK)
+        return pltpu.make_async_remote_copy(
+            src_ref=guest.at[visit],
+            dst_ref=held.at[visit + 1, rows],
+            send_sem=guest_send.at[visit],
+            recv_sem=recv_sem.at[visit, chunk],
+            device_id=guest_to,
+            device_id_type=MESH,
+        )
+
+    def serve(visit):
+        @pl.when(is_host)
+        def _():
+            send_guest(visit, 0).wait_recv()
+            guest_on(visit).start()
+
+    def dispatch(visit, chunk):
+        if visit < VISITS - 2:
+            apart = is_last & odd & (chunk >= GBASE) & (chunk < GBASE + GUESTS)
+
+            @pl.when(apart)
+            def _():
+                send_guest(visit, jnp.clip(chunk - GBASE, 0, GUESTS - 1)).start()
+
+            @pl.when(jnp.logical_not(apart))
+            def _():
+                send(visit, chunk).start()
+        elif visit == VISITS - 2:
+            @pl.when(is_last)
+            def _():
+                send_around(chunk).start()
+
+            @pl.when(jnp.logical_not(is_last))
+            def _():
+                send(visit, chunk).start()
+
+    def forward(chunk):
+        @pl.when(is_first)
+        def _():
+            send_around(chunk).wait_recv()
+            pass_on(chunk).start()
 
     def update(visit, chunk):
         rows = pl.ds(pl.multiple_of(chunk * CHUNK, CHUNK), CHUNK)
@@ -90,22 +216,30 @@
         load_obs(visit).wait()
 
         if visit == 0:
-            @pl.loop(0, chunks)
-            def _(chunk):
-                update(0, chunk)
-
-            pl.semaphore_wait(barrier, 4)
-
-            @pl.loop(0, chunks)
-            def _(chunk):
-                send(0, chunk).start()
-        else:
-            @pl.loop(0, chunks)
-            def _(chunk, visit=visit):
+            update(0, 0)
+            meet()
+            dispatch(0, 0)
+        elif visit == VISITS - 1:
+            for chunk in range(min(AHEAD, RELAYED)):
+                forward(chunk)
+
+        @pl.loop(1 if visit == 0 else 0, chunks)
+        def _(chunk, visit=visit):
+            if visit == VISITS - 1 and AHEAD < RELAYED:
+                @pl.when(chunk + AHEAD < RELAYED)
+                def _():
+                    forward(chunk + AHEAD)
+
+            if visit:
                 send(visit - 1, chunk).wait_recv()
-                update(visit, chunk)
-                if visit < VISITS - 1:
-                    send(visit, chunk).start()
+            update(visit, chunk)
+            dispatch(visit, chunk)
+
+        if visit == 0:
+            serve(0)
+            serve(1)
+        elif visit == 1:
+            serve(2)
 
         current = frames[...]
         updated = current + step_frames * (total[...] - decay_weight * current)
@@ -119,6 +253,16 @@
         def _(chunk, visit=visit):
             send(visit, chunk).wait_send()
 
+    @pl.when(is_host)
+    def _():
+        for visit in range(VISITS - 2):
+            guest_on(visit).wait_send()
+
+    @pl.when(is_first)
+    def _():
+        for chunk in range(RELAYED):
+            pass_on(chunk).wait_send()
+
 
 def solution(mesh):
     n_blk, n_wide = mesh.shape["blk"], mesh.shape["wide"]
@@ -129,10 +273,10 @@
         return tuple(pl.pallas_call(
             functools.partial(kernel, n_blk, n_wide),
             out_shape=(
-                jax.ShapeDtypeStruct(frame_factors.shape, frame_factors.dtype),
-                jax.ShapeDtypeStruct(pixel_factors.shape, pixel_factors.dtype),
+                pltpu.VMEM(frame_factors.shape, frame_factors.dtype),
+                pltpu.VMEM(pixel_factors.shape, pixel_factors.dtype),
             ),
-            in_specs=[pl.BlockSpec(memory_space=pl.ANY)] * 4,
+            in_specs=[pl.BlockSpec(memory_space=pltpu.HBM)] * 4,
             out_specs=(pl.BlockSpec(memory_space=pltpu.VMEM),) * 2,
             scratch_shapes=[
                 pltpu.VMEM(observed.shape, observed.dtype),
@@ -142,14 +286,20 @@
                 pltpu.VMEM(frame_factors.shape, jnp.float32),
                 pltpu.VMEM((VISITS, width, rank), jnp.bfloat16),
                 pltpu.VMEM((VISITS - 1, width, rank), jnp.bfloat16),
+                pltpu.VMEM((max(RELAYED, 1) * CHUNK, rank), jnp.bfloat16),
                 pltpu.SemaphoreType.DMA((3 + VISITS,)),
                 pltpu.SemaphoreType.DMA((VISITS - 1, chunks)),
                 pltpu.SemaphoreType.DMA((VISITS - 1, chunks)),
+                pltpu.SemaphoreType.DMA((chunks,)),
+                pltpu.SemaphoreType.DMA((chunks,)),
+                pltpu.VMEM((VISITS - 2, CHUNK, rank), jnp.bfloat16),
+                pltpu.SemaphoreType.DMA((VISITS - 2,)),
+                pltpu.SemaphoreType.DMA((VISITS - 2,)),
             ],
             compiler_params=pltpu.CompilerParams(
-                collective_id=0, has_side_effects=True
+                collective_id=0, has_side_effects=True, vmem_limit_bytes=20 << 20
             ),
-        )(observed, mask_bits, frame_factors, pixel_factors))
+        )(*(pltpu.with_memory_space_constraint(x, pltpu.HBM) for x in (observed, mask_bits, frame_factors, pixel_factors))))
 
     spec = P(("blk", "wide"), None)
     return jax.shard_map(

time: 72.5 us -> 61 us (0.84)
  Pallas kernels: 68.1 us -> 58.7 us
  local copies, waits for them, and re-layouts: 3.54 us -> 1.5 us
    pallas_call x1, Pallas kernels: 68.1 us -> 58.7 us  [body(): pl.pallas_call(functools.partial(kernel, n_blk, n_wide), out_shape=(pltpu...]
    unnamed x2, local copies, waits for them, and re-layouts: 3.54 us -> 1.5 us
where the time goes in v2:
time: 61 us; the launch traced here: 60.8 us
  Pallas kernels  58.7 us (96%)
  local copies, waits for them, and re-layouts  1.5 us (2%)
  between operations  0.64 us (1%)
    pallas_call x1, Pallas kernels, body(): pl.pallas_call(functools.partial(kernel, n_blk, n_wide), out_shape=(pltpu...  58.7 us
    unnamed x2, local copies, waits for them, and re-layouts  1.5 us

profile of v2, /device:TPU:16, one launch (start us, length us, event | category | flops | bytes accessed | tf_op | source)
XLA Modules:
  0.0 60.8 jit_solution(9584505573534098708)
XLA Ops:
  0.6 58.7 %shard_map.59 = (f32[256,256]{1,0:T(8,128)S(1)}, bf16[1024,256]{1,0:T(8,128)(2,1)S(1)}) custom-call(bf16[256,5120]{1,0:T(8,128)(2,1)} %obs_hbm.1, s32[256,640]{1,0:T(8,128)} %bits_hbm.1, f32[256,256]{1,0:T(8,128)} %frames_hbm.1, bf16[1024,256]{1,0:T(8,128)(2,1)} %pixels_hbm.1), custom_call_target="tpu_custom_call" | custom-call | tf_op jit(solution)/shard_map/pallas_call | solution.py:273
  59.3 0.7 %copy.8 = f32[256,256]{1,0:T(8,128)} copy(f32[256,256]{1,0:T(8,128)S(1)} %get-tuple-element.2) | data formatting | bytes 524288
  60.0 0.8 %copy.9 = bf16[1024,256]{1,0:T(8,128)(2,1)} copy(bf16[1024,256]{1,0:T(8,128)(2,1)S(1)} %get-tuple-element.3) | data formatting | bytes 1048576

commit v3 on v2

--- a/solution.py
+++ b/solution.py
@@ -11,10 +11,10 @@
 LANES = 128
 CHUNK = 128
 RUN = 8
-RELAYED = 8
-AHEAD = 5
-GBASE = 5
-GUESTS = 3
+RELAYED = 5
+AHEAD = 4
+GBASE = 6
+GUESTS = 2
 MESH = pl.DeviceIdType.MESH
 
 step_frames = 0.01
@@ -47,11 +47,8 @@
     def greet(peer):
         pl.semaphore_signal(barrier, inc=1, device_id=peer, device_id_type=MESH)
 
-    greet(last_blk)
-
-    @pl.when(jnp.logical_not(is_first))
-    def _():
-        greet(left)
+    for peer in (last_blk, left):
+        greet(peer)
 
     odd = lax.rem(i, 2) == 1
     even = jnp.logical_not(odd)
@@ -78,18 +75,29 @@
         greet(last_run)
 
     def meet():
-        extra = jnp.where(is_host | is_first, 1, jnp.where(is_last & odd, GUESTS, 0))
+        extra = jnp.where(is_host | is_first, 1, jnp.where(is_last, 1 + jnp.where(odd, GUESTS, 0), 0))
         pl.semaphore_wait(barrier, 2 + extra)
 
     def load(source, target, index):
         return pltpu.make_async_copy(source, target, load_sem.at[index])
 
     def load_obs(visit):
-        columns = pl.ds(visit * width, width)
+        start = CHUNK if visit == 0 else visit * width
+        columns = pl.ds(start, (visit + 1) * width - start)
         return load(obs_hbm.at[:, columns], obs.at[:, columns], 3 + visit)
 
-    first = [load(frames_hbm, frames, 0), load(pixels_hbm, held.at[0], 1), load(bits_hbm, bits, 2)]
-    for copy in first:
+    head, tail, lane_tail = pl.ds(0, CHUNK), pl.ds(CHUNK, width - CHUNK), pl.ds(LANES, bits.shape[1] - LANES)
+    first = [
+        load(frames_hbm, frames, 0),
+        load(pixels_hbm.at[head], held.at[0, head], 1),
+        load(bits_hbm.at[:, pl.ds(0, LANES)], bits.at[:, pl.ds(0, LANES)], 2),
+        load(obs_hbm.at[:, head], obs.at[:, head], 3 + VISITS),
+    ]
+    second = [
+        load(pixels_hbm.at[tail], held.at[0, tail], 4 + VISITS),
+        load(bits_hbm.at[:, lane_tail], bits.at[:, lane_tail], 5 + VISITS),
+    ]
+    for copy in first + second:
         copy.start()
     for visit in range(VISITS):
         load_obs(visit).start()
@@ -172,11 +180,13 @@
             def _():
                 send(visit, chunk).start()
         elif visit == VISITS - 2:
-            @pl.when(is_last)
+            around = is_last & (chunk < RELAYED)
+
+            @pl.when(around)
             def _():
                 send_around(chunk).start()
 
-            @pl.when(jnp.logical_not(is_last))
+            @pl.when(jnp.logical_not(around))
             def _():
                 send(visit, chunk).start()
 
@@ -213,13 +223,16 @@
     for visit in range(VISITS):
         low[...] = frames[...].astype(jnp.bfloat16)
         total[...] = jnp.zeros_like(total)
-        load_obs(visit).wait()
 
         if visit == 0:
             update(0, 0)
             meet()
             dispatch(0, 0)
-        elif visit == VISITS - 1:
+            for copy in second:
+                copy.wait()
+        load_obs(visit).wait()
+
+        if visit == VISITS - 1:
             for chunk in range(min(AHEAD, RELAYED)):
                 forward(chunk)
 
@@ -264,13 +277,38 @@
             pass_on(chunk).wait_send()
 
 
+def store_kernel(frames, pixels, frames_out, pixels_out, sem):
+    copies = [
+        pltpu.make_async_copy(frames, frames_out, sem.at[0]),
+        pltpu.make_async_copy(pixels, pixels_out, sem.at[1]),
+    ]
+    for copy in copies:
+        copy.start()
+    for copy in copies:
+        copy.wait()
+
+
+def store(frames, pixels):
+    return pl.pallas_call(
+        store_kernel,
+        out_shape=(
+            jax.ShapeDtypeStruct(frames.shape, frames.dtype),
+            jax.ShapeDtypeStruct(pixels.shape, pixels.dtype),
+        ),
+        in_specs=[pl.BlockSpec(memory_space=pltpu.VMEM)] * 2,
+        out_specs=(pl.BlockSpec(memory_space=pl.ANY),) * 2,
+        scratch_shapes=[pltpu.SemaphoreType.DMA((2,))],
+        compiler_params=pltpu.CompilerParams(vmem_limit_bytes=8 << 20),
+    )(frames, pixels)
+
+
 def solution(mesh):
     n_blk, n_wide = mesh.shape["blk"], mesh.shape["wide"]
 
     def body(observed, mask_bits, frame_factors, pixel_factors):
         width, rank = pixel_factors.shape
         chunks = width // CHUNK
-        return tuple(pl.pallas_call(
+        return store(*pl.pallas_call(
             functools.partial(kernel, n_blk, n_wide),
             out_shape=(
                 pltpu.VMEM(frame_factors.shape, frame_factors.dtype),
@@ -287,7 +325,7 @@
                 pltpu.VMEM((VISITS, width, rank), jnp.bfloat16),
                 pltpu.VMEM((VISITS - 1, width, rank), jnp.bfloat16),
                 pltpu.VMEM((max(RELAYED, 1) * CHUNK, rank), jnp.bfloat16),
-                pltpu.SemaphoreType.DMA((3 + VISITS,)),
+                pltpu.SemaphoreType.DMA((6 + VISITS,)),
                 pltpu.SemaphoreType.DMA((VISITS - 1, chunks)),
                 pltpu.SemaphoreType.DMA((VISITS - 1, chunks)),
                 pltpu.SemaphoreType.DMA((chunks,)),

time: 61 us -> 57.8 us (0.948)
  the two profiles are of different devices: /device:TPU:16 before, /device:TPU:8 now
where the time goes in v3:
time: 57.8 us; the launch traced here: 57.7 us
  Pallas kernels  57.1 us (99%)
  between operations  0.64 us (1%)
    pallas_call x1, Pallas kernels, body(): pl.pallas_call(functools.partial(kernel, n_blk, n_wide), out_shape=(pltpu...  56.2 us

profile of v3, /device:TPU:8, one launch (start us, length us, event | category | flops | bytes accessed | tf_op | source)
XLA Modules:
  0.0 57.7 jit_solution(14500375193451317469)
XLA Ops:
  0.6 56.2 %shard_map.59 = (f32[256,256]{1,0:T(8,128)S(1)}, bf16[1024,256]{1,0:T(8,128)(2,1)S(1)}) custom-call(bf16[256,5120]{1,0:T(8,128)(2,1)} %obs_hbm.1, s32[256,640]{1,0:T(8,128)} %bits_hbm.1, f32[256,256]{1,0:T(8,128)} %frames_hbm.1, bf16[1024,256]{1,0:T(8,128)(2,1)} %pixels_hbm.1), custom_call_target="tpu_custom_call" | custom-call | tf_op jit(solution)/shard_map/pallas_call | solution.py:311
  56.8 0.9 %shard_map.60 = (f32[256,256]{1,0:T(8,128)}, bf16[1024,256]{1,0:T(8,128)(2,1)}) custom-call(f32[256,256]{1,0:T(8,128)S(1)} %get-tuple-element.4.frames, bf16[1024,256]{1,0:T(8,128)(2,1)S(1)} %get-tuple-element.5.pixels), custom_call_target="tpu_custom_call" | custom-call | tf_op jit(solution)/shard_map/pallas_call | solution.py:292

commit v4 on v3

--- a/solution.py
+++ b/solution.py
@@ -11,10 +11,10 @@
 LANES = 128
 CHUNK = 128
 RUN = 8
-RELAYED = 5
-AHEAD = 4
-GBASE = 6
-GUESTS = 2
+RELAYED = 3
+AHEAD = 3
+GBASE = 5
+GUESTS = 3
 MESH = pl.DeviceIdType.MESH
 
 step_frames = 0.01

time: 57.8 us -> 57.5 us (level)
  the two profiles are of different devices: /device:TPU:8 before, /device:TPU:1 now
where the time goes in v4:
time: 57.5 us; the launch traced here: 57.4 us
  Pallas kernels  56.8 us (99%)
  between operations  0.64 us (1%)
    pallas_call x1, Pallas kernels, body(): pl.pallas_call(functools.partial(kernel, n_blk, n_wide), out_shape=(pltpu...  55.9 us

profile of v4, /device:TPU:1, one launch (start us, length us, event | category | flops | bytes accessed | tf_op | source)
XLA Modules:
  0.0 57.4 jit_solution(13361281312953586946)
XLA Ops:
  0.6 55.9 %shard_map.59 = (f32[256,256]{1,0:T(8,128)S(1)}, bf16[1024,256]{1,0:T(8,128)(2,1)S(1)}) custom-call(bf16[256,5120]{1,0:T(8,128)(2,1)} %obs_hbm.1, s32[256,640]{1,0:T(8,128)} %bits_hbm.1, f32[256,256]{1,0:T(8,128)} %frames_hbm.1, bf16[1024,256]{1,0:T(8,128)(2,1)} %pixels_hbm.1), custom_call_target="tpu_custom_call" | custom-call | tf_op jit(solution)/shard_map/pallas_call | solution.py:311
  56.5 0.9 %shard_map.60 = (f32[256,256]{1,0:T(8,128)}, bf16[1024,256]{1,0:T(8,128)(2,1)}) custom-call(f32[256,256]{1,0:T(8,128)S(1)} %get-tuple-element.4.frames, bf16[1024,256]{1,0:T(8,128)(2,1)S(1)} %get-tuple-element.5.pixels), custom_call_target="tpu_custom_call" | custom-call | tf_op jit(solution)/shard_map/pallas_call | solution.py:292
